TPU v7x, 32 devices: a whole 2x2x4 slice. The times are simulated.
32 devices in a mesh: grp: 2 (over y), row: 4 (over z), col: 2 (over x), rep: 2 (over core).
Axes of the slice: x: 2, y: 2, z: 4, core: 2. Of those that a mesh axis runs over, the one named last changes fastest.
Arguments:
- shard_rows: bfloat16 [11520, 512], P(('grp', 'row', 'col', 'rep')), parts along dimension 0, may hold values from -24 to 24
- row_position: int32 [11520], P(('grp', 'row', 'col', 'rep')), parts along dimension 0, may hold values from 0 to 3071, as said below
- shard_count: int32 [32], P(('grp', 'row', 'col', 'rep')), parts along dimension 0, may hold values from 1 to 360, as said below
Outputs:
- max_similarity: float32 [6144], P(('grp', 'row', 'col', 'rep')), parts along dimension 0
There are 2 independent parts, one for each index of `grp`. A program takes and returns all parts, laid end to end along the dimension named above; each array names one. Nothing has to cross between parts.
Inputs may be any that keep to these rules, and one draw needn't show every extreme that they name: `row_position`: row j of shard s is used when j < shard_count[s]; the used rows of all shards hold every position 0 to 3071 once, unused rows hold arbitrary positions. At most 24 used rows of one shard have positions in one aligned run of 192 positions, and some shard reaches 24. `shard_count`: the counts sum to 3072.
All inputs are finite; a program needn't handle non-finite values.
Results may differ from a plain program's by a relative error of at most 0.00063.
Values may be sent and summed in bfloat16 or wider, within the bound.
A program may use at most 64 MiB of HBM per device.

v0:
```python
import math
import jax
import jax.numpy as jnp
from jax import lax
from jax.sharding import PartitionSpec as P

OWN = 192


def normalize(owned_rows):
    widened = owned_rows.astype(jnp.float32)
    return (widened / jnp.sqrt(jnp.sum(widened * widened, 1, keepdims=True) + 1e-06)).astype(
        jnp.bfloat16
    )


def body(shard_rows, row_position, shard_count):
    row_devices = lax.axis_size("row")
    cross_devices = lax.axis_size(("col", "rep"))
    all_shards = row_devices * cross_devices
    per_owner = OWN
    owner_load = max(1, per_owner // all_shards)
    slot_count = 2 * owner_load
    block_rows = per_owner * cross_devices
    capacity, feature = shard_rows.shape
    row_place = lax.axis_index("row")
    cross_place = lax.axis_index(("col", "rep"))
    is_used = jnp.arange(capacity) < shard_count[0]
    position = jnp.where(is_used, row_position, 0)
    owner_first = position // per_owner
    one_hot = jnp.logical_and(
        owner_first[:, None] == jnp.arange(all_shards)[None, :], is_used[:, None]
    ).astype(jnp.int32)
    ranking = jnp.sum(jnp.cumsum(one_hot, 0) * one_hot, 1) - 1
    target = jnp.where(is_used, owner_first * slot_count + ranking, all_shards * slot_count)
    packed = (
        jnp.zeros((all_shards * slot_count, feature), shard_rows.dtype)
        .at[target]
        .set(shard_rows, mode="drop")
    )
    placed = (
        jnp.full((all_shards * slot_count,), -1, jnp.int32).at[target].set(position, mode="drop")
    )
    first_packed = packed.reshape(row_devices, cross_devices, slot_count, feature)
    first_placed = placed.reshape(row_devices, cross_devices, slot_count)
    own_offset = row_place * block_rows + cross_place * per_owner
    received = (
        lax.all_to_all(
            lax.all_to_all(first_packed, "row", split_axis=0, concat_axis=0, tiled=True),
            ("col", "rep"),
            split_axis=1,
            concat_axis=1,
            tiled=True,
        ),
        lax.all_to_all(
            lax.all_to_all(first_placed, "row", split_axis=0, concat_axis=0, tiled=True),
            ("col", "rep"),
            split_axis=1,
            concat_axis=1,
            tiled=True,
        ),
    )
    flat_rows = received[0].reshape(-1, feature)
    flat_places = received[1].reshape(-1)
    local_index = jnp.where(flat_places >= 0, flat_places - own_offset, per_owner)
    owned_rows = (
        jnp.zeros((per_owner, feature), flat_rows.dtype).at[local_index].set(flat_rows, mode="drop")
    )
    row_owned = normalize(owned_rows)
    row_block = lax.all_gather(row_owned, ("col", "rep"), axis=0, tiled=True)
    column_index = jnp.arange(block_rows)
    column_block = lax.all_gather(row_owned, "row", axis=0, tiled=True)
    column_places = (
        column_index // per_owner * block_rows + cross_place * per_owner + column_index % per_owner
    )
    row_step = math.gcd(block_rows, 512)
    column_step = math.gcd(block_rows, 1024)

    def row_maxima(inputs):
        row_tile, row_start = inputs
        row_global = row_place * block_rows + row_start + jnp.arange(row_step)
        running = jnp.full((row_step,), -4.0, jnp.float32)
        for column_turn in range(block_rows // column_step):
            column_tile = column_block[column_turn * column_step : (column_turn + 1) * column_step]
            scores = jnp.einsum(
                "rd,cd->rc", row_tile, column_tile, preferred_element_type=jnp.float32
            )
            column_global = column_places[
                column_turn * column_step : (column_turn + 1) * column_step
            ]
            scores = jnp.where(row_global[:, None] == column_global[None, :], -4.0, scores)
            running = jnp.maximum(running, jnp.max(scores, 1))
        return running

    starts = jnp.arange(block_rows // row_step, dtype=jnp.int32) * row_step
    maxima = lax.map(row_maxima, (row_block.reshape(-1, row_step, feature), starts)).reshape(
        block_rows
    )
    combined = lax.pmax(maxima, ("col", "rep"))
    return lax.dynamic_slice_in_dim(combined, cross_place * per_owner, per_owner)


def solution(mesh):
    return jax.shard_map(
        body,
        mesh=mesh,
        in_specs=(
            P(("grp", "row", "col", "rep"), None),
            P(("grp", "row", "col", "rep")),
            P(("grp", "row", "col", "rep")),
        ),
        out_specs=P(("grp", "row", "col", "rep")),
        check_vma=False,
    )
```

profile of v0, /device:TPU:0, one launch (start us, length us, event | category | flops | bytes accessed | tf_op | source)
XLA Modules:
  0.0 92.6 jit_solution(1535740901777857113)
XLA Ops:
  0.7 0.0 copy-start
  0.7 0.7 copy-done
  1.4 0.9 reduce-window.6
  2.3 0.2 slice_reduce_fusion
  2.5 0.1 bitcast_bitcast_fusion
  2.6 2.9 %scatter_custom_fusion = s32[384]{0:T(512)S(1)} fusion(s32[360]{0:T(512)S(1)} %compare_select_fusion.1, s32[360]{0:T(512)S(1)} %get-tuple-element.104, s32[]{:T(128)} %constant.84.clone.1), kind=kCustom, calls=%fused_computation.67 | custom fusion | bytes 1540 | tf_op jit(solution)/shard_map/scatter | solution.py:42
  5.5 0.7 reshape.115
  6.2 6.3 %all-to-all-start = ((s32[4,4,24]{2,1,0:T(4,128)}), s32[4,4,24]{2,1,0:T(4,128)S(1)}, u32[]{:S(2)}, u32[]{:S(2)}) async-start(s32[4,4,24]{2,1,0:T(4,128)} %reshape.115), calls=%async_computation | async-start | bytes 16384 | tf_op jit(solution)/shard_map/all_to_all | solution.py:56
  12.6 3.0 %scatter_custom_fusion.1 = bf16[384,512]{1,0:T(8,128)(2,1)} fusion(s32[360]{0:T(512)S(1)} %compare_select_fusion.1, bf16[360,512]{1,0:T(8,128)(2,1)} %param.5, bf16[]{:T(256)} %constant.83.clone.1), kind=kCustom, calls=%fused_computation.27 | custom fusion | bytes 393728 | tf_op jit(solution)/shard_map/scatter | solution.py:39
  15.6 2.6 %all-to-all-done = s32[4,4,24]{2,1,0:T(4,128)S(1)} async-done(((s32[4,4,24]{2,1,0:T(4,128)}), s32[4,4,24]{2,1,0:T(4,128)S(1)}, u32[]{:S(2)}, u32[]{:S(2)}) %all-to-all-start) | async-done | bytes 1568 | tf_op jit(solution)/shard_map/all_to_all | solution.py:56
  18.2 3.5 %all-to-all-start.2 = ((bf16[4,4,24,512]{3,2,1,0:T(8,128)(2,1)}), bf16[4,4,24,512]{3,2,1,0:T(8,128)(2,1)S(1)}, u32[]{:S(2)}, u32[]{:S(2)}) async-start(bf16[4,4,24,512]{3,2,1,0:T(8,128)(2,1)} %bitcast.5), calls=%async_computation.2 | async-start | bytes 786432 | tf_op jit(solution)/shard_map/all_to_all | solution.py:49
  21.6 0.6 copy.17
  22.2 9.9 %all-to-all-done.2 = bf16[4,4,24,512]{3,2,1,0:T(8,128)(2,1)S(1)} async-done(((bf16[4,4,24,512]{3,2,1,0:T(8,128)(2,1)}), bf16[4,4,24,512]{3,2,1,0:T(8,128)(2,1)S(1)}, u32[]{:S(2)}, u32[]{:S(2)}) %all-to-all-start.2) | async-done | bytes 393248 | tf_op jit(solution)/shard_map/all_to_all | solution.py:49
  32.1 3.2 %all-to-all-start.1 = ((s32[4,4,24]{2,0,1:T(4,128)}), s32[4,4,24]{2,0,1:T(4,128)S(1)}, u32[]{:S(2)}, u32[]{:S(2)}) async-start(s32[4,4,24]{2,0,1:T(4,128)} %copy.17), calls=%async_computation.1 | async-start | bytes 16384 | tf_op jit(solution)/shard_map/all_to_all | solution.py:55
  35.4 0.8 copy.19
  36.2 3.0 %all-to-all-done.1 = s32[4,4,24]{2,0,1:T(4,128)S(1)} async-done(((s32[4,4,24]{2,0,1:T(4,128)}), s32[4,4,24]{2,0,1:T(4,128)S(1)}, u32[]{:S(2)}, u32[]{:S(2)}) %all-to-all-start.1) | async-done | bytes 1568 | tf_op jit(solution)/shard_map/all_to_all | solution.py:55
  39.1 3.5 %all-to-all-start.3 = ((bf16[4,4,24,512]{3,2,0,1:T(8,128)(2,1)}), bf16[4,4,24,512]{3,2,0,1:T(8,128)(2,1)S(1)}, u32[]{:S(2)}, u32[]{:S(2)}) async-start(bf16[4,4,24,512]{3,2,0,1:T(8,128)(2,1)} %copy.19), calls=%async_computation.3 | async-start | bytes 786432 | tf_op jit(solution)/shard_map/all_to_all | solution.py:48
  42.6 0.1 select_n.78
  42.7 7.3 %all-to-all-done.3 = bf16[4,4,24,512]{3,2,0,1:T(8,128)(2,1)S(1)} async-done(((bf16[4,4,24,512]{3,2,0,1:T(8,128)(2,1)}), bf16[4,4,24,512]{3,2,0,1:T(8,128)(2,1)S(1)}, u32[]{:S(2)}, u32[]{:S(2)}) %all-to-all-start.3) | async-done | bytes 393248 | tf_op jit(solution)/shard_map/all_to_all | solution.py:48
  50.0 2.0 %scatter_custom_fusion.2 = bf16[192,512]{1,0:T(8,128)(2,1)S(1)} fusion(s32[384]{0:T(512)S(1)} %fusion.35, bf16[384,512]{1,0:T(8,128)(2,1)S(1)} %bitcast.40, bf16[]{:T(256)} %constant.83.clone.1), kind=kCustom, calls=%fused_computation.29 | custom fusion | bytes 196610 | tf_op jit(solution)/shard_map/scatter | solution.py:67
  52.0 0.1 fusion.15
  52.2 0.1 fusion.16
  52.3 18.0 %all_gather.7 = bf16[768,512]{1,0:T(8,128)(2,1)S(1)} all-gather(bf16[192,512]{1,0:T(8,128)(2,1)S(1)} %fusion.16), channel_id=1, replica_groups=mesh['grp'=2,'row'=4,'col'=2,'rep'=2] {'row'}, dimensions={0}, use_global_device_ids=true | all-gather | bytes 983040 | tf_op jit(solution)/shard_map/all_gather | solution.py:72
  70.3 7.5 %all_gather.6 = bf16[768,512]{1,0:T(8,128)(2,1)S(1)} all-gather(bf16[192,512]{1,0:T(8,128)(2,1)S(1)} %fusion.16), channel_id=1, replica_groups=mesh['grp'=2,'row'=4,'col'=2,'rep'=2] {'col','rep'}, dimensions={0}, use_global_device_ids=true | all-gather | bytes 983040 | tf_op jit(solution)/shard_map/all_gather | solution.py:70
  77.8 6.9 %while.12 = (s32[]{:T(128)}, f32[3,256]{1,0:T(4,128)S(1)}, s32[3]{0:T(128)S(1)}, s32[]{:T(128)}, s32[768]{0:T(1024)S(1)}, /*index=5*/bf16[3,256,512]{2,1,0:T(8,1...) while((s32[]{:T(128)}, f32[3,256]{1,0:T(4,128)S(1)}, s32[3]{0:T(128)S(1)}, s32[]{:T(128)}, ...), condition=%wide.region_11.12_spmd, body=%wide.region_7.11_spmd.sunk | while | flops 201916672 | bytes 1595529 | solution.py:96
  77.8 0.7 dynamic_slice.35
  79.1 0.3 fusion.58
  79.4 0.3 fusion.57
  79.7 0.3 fusion.56
  80.1 0.7 dynamic_slice.35
  81.4 0.3 fusion.58
  81.7 0.3 fusion.57
  82.0 0.3 fusion.56
  82.3 0.7 dynamic_slice.35
  83.7 0.3 fusion.58
  84.0 0.3 fusion.57
  84.3 0.3 fusion.56
  84.6 7.3 %pmax.7 = f32[768]{0:T(1024)S(1)} all-reduce(f32[768]{0:T(1024)S(1)} %reshape.119), channel_id=1, replica_groups=mesh['grp'=2,'row'=4,'col'=2,'rep'=2] {'col','rep'}, use_global_device_ids=true, to_apply=%region_12.13 | all-reduce | flops 768 | bytes 6144 | tf_op jit(solution)/shard_map/pmax | solution.py:99
  91.9 0.6 dynamic_slice.15
  (25 shorter events, 0.4 us)
Async XLA Ops:
  0.7 0.7 copy-start
  6.2 11.9 %all-to-all-start = ((s32[4,4,24]{2,1,0:T(4,128)}), s32[4,4,24]{2,1,0:T(4,128)S(1)}, u32[]{:S(2)}, u32[]{:S(2)}) async-start(s32[4,4,24]{2,1,0:T(4,128)} %reshape.115), calls=%async_computation | async-start | bytes 16384 | tf_op jit(solution)/shard_map/all_to_all | solution.py:56
  18.2 14.0 %all-to-all-start.2 = ((bf16[4,4,24,512]{3,2,1,0:T(8,128)(2,1)}), bf16[4,4,24,512]{3,2,1,0:T(8,128)(2,1)S(1)}, u32[]{:S(2)}, u32[]{:S(2)}) async-start(bf16[4,4,24,512]{3,2,1,0:T(8,128)(2,1)} %bitcast.5), calls=%async_computation.2 | async-start | bytes 786432 | tf_op jit(solution)/shard_map/all_to_all | solution.py:49
  32.1 7.0 %all-to-all-start.1 = ((s32[4,4,24]{2,0,1:T(4,128)}), s32[4,4,24]{2,0,1:T(4,128)S(1)}, u32[]{:S(2)}, u32[]{:S(2)}) async-start(s32[4,4,24]{2,0,1:T(4,128)} %copy.17), calls=%async_computation.1 | async-start | bytes 16384 | tf_op jit(solution)/shard_map/all_to_all | solution.py:55
  39.1 10.9 %all-to-all-start.3 = ((bf16[4,4,24,512]{3,2,0,1:T(8,128)(2,1)}), bf16[4,4,24,512]{3,2,0,1:T(8,128)(2,1)S(1)}, u32[]{:S(2)}, u32[]{:S(2)}) async-start(bf16[4,4,24,512]{3,2,0,1:T(8,128)(2,1)} %copy.19), calls=%async_computation.3 | async-start | bytes 786432 | tf_op jit(solution)/shard_map/all_to_all | solution.py:48
where the time goes:
time: 93.1 us; the launch traced here: 92.6 us
  blocking collectives  32.8 us (35%)
  waiting for transfers between devices  22.7 us (24%)
  starting transfers between devices  16.5 us (18%)
  local copies, waits for them, and re-layouts  13.7 us (15%)
  matrix products  2.53 us (3%)
  loops' own time  2.18 us (2%)
  other arithmetic  1.38 us (1%)
    all_gather x1, blocking collectives, body(): column_block = lax.all_gather(row_owned, 'row', axis=0, tiled=True)  18 us
    all_to_all x1, waiting for transfers between devices, body(): lax.all_to_all(first_packed, 'row', split_axis=0, concat_axis=0, tiled=True)  9.87 us
    all_gather x1, blocking collectives, body(): row_block = lax.all_gather(row_owned, ('col', 'rep'), axis=0, tiled=True)  7.46 us
    pmax x1, blocking collectives, body(): combined = lax.pmax(maxima, ('col', 'rep'))  7.28 us
    all_to_all x1, waiting for transfers between devices, body(): lax.all_to_all(lax.all_to_all(first_packed, 'row', split_axis=0, concat_a...  7.27 us
    all_to_all x1, starting transfers between devices, body(): lax.all_to_all(first_placed, 'row', split_axis=0, concat_axis=0, tiled=True)  6.32 us
    all_to_all x1, starting transfers between devices, body(): lax.all_to_all(lax.all_to_all(first_packed, 'row', split_axis=0, concat_a...  3.46 us
    all_to_all x1, starting transfers between devices, body(): lax.all_to_all(first_packed, 'row', split_axis=0, concat_axis=0, tiled=True)  3.46 us
  transfers between devices with their start and end apart: 4, of which 4 were waited for; matrix products, arithmetic and copies ran while one was open for 5% of the time, Pallas kernels for 0%

commit v1 on v0

--- a/solution.py
+++ b/solution.py
@@ -69,7 +69,12 @@
     row_owned = normalize(owned_rows)
     row_block = lax.all_gather(row_owned, ("col", "rep"), axis=0, tiled=True)
     column_index = jnp.arange(block_rows)
-    column_block = lax.all_gather(row_owned, "row", axis=0, tiled=True)
+    ring = [row_owned]
+    for hop in range(3):
+        ring.append(lax.ppermute(ring[-1], "row", [(dev, (dev + 1) % 4) for dev in range(4)]))
+    column_block = jnp.roll(
+        jnp.concatenate(ring[::-1], axis=0), (lax.axis_index("row") + 1) * ring[0].shape[0], axis=0
+    )
     column_places = (
         column_index // per_owner * block_rows + cross_place * per_owner + column_index % per_owner
     )

time: 93.1 us -> 91.4 us (0.982)
  blocking collectives: 32.8 us -> 14.7 us
  waiting for transfers between devices: 22.7 us -> 38.4 us
    all_gather x1 -> x0, blocking collectives: 18 us -> none  [body(): column_block = lax.all_gather(row_owned, 'row', axis=0, tiled=True)]
    ppermute x0 -> x3, waiting for transfers between devices: none -> 15.6 us  [body(): lax.ppermute(ring[-1], 'row', [(dev, (dev + 1) % 4) for dev in range(4)])]
  transfers between devices with their start and end apart: 4 -> 7, of which waited for: 4 -> 6; matrix products, arithmetic and copies ran while one was open for 5% -> 5% of each run, Pallas kernels for 0% -> 0%
where the time goes in v1:
time: 91.4 us; the launch traced here: 90.9 us
  waiting for transfers between devices  38.4 us (42%)
  starting transfers between devices  16.5 us (18%)
  blocking collectives  14.7 us (16%)
  local copies, waits for them, and re-layouts  13.4 us (15%)
  matrix products  2.53 us (3%)
  other arithmetic  2.27 us (2%)
  loops' own time  2.2 us (2%)
    ppermute x3, waiting for transfers between devices, body(): lax.ppermute(ring[-1], 'row', [(dev, (dev + 1) % 4) for dev in range(4)])  15.6 us
    all_to_all x1, waiting for transfers between devices, body(): lax.all_to_all(first_packed, 'row', split_axis=0, concat_axis=0, tiled=True)  9.9 us
    all_gather x1, blocking collectives, body(): row_block = lax.all_gather(row_owned, ('col', 'rep'), axis=0, tiled=True)  7.9 us
    all_to_all x1, waiting for transfers between devices, body(): lax.all_to_all(lax.all_to_all(first_packed, 'row', split_axis=0, concat_a...  7.26 us
    pmax x1, blocking collectives, body(): combined = lax.pmax(maxima, ('col', 'rep'))  6.83 us
    all_to_all x1, starting transfers between devices, body(): lax.all_to_all(first_placed, 'row', split_axis=0, concat_axis=0, tiled=True)  6.32 us
    all_to_all x1, starting transfers between devices, body(): lax.all_to_all(first_packed, 'row', split_axis=0, concat_axis=0, tiled=True)  3.46 us
    all_to_all x1, starting transfers between devices, body(): lax.all_to_all(lax.all_to_all(first_packed, 'row', split_axis=0, concat_a...  3.46 us
  transfers between devices with their start and end apart: 7, of which 6 were waited for; matrix products, arithmetic and copies ran while one was open for 5% of the time, Pallas kernels for 0%

profile of v1, /device:TPU:0, one launch (start us, length us, event | category | flops | bytes accessed | tf_op | source)
XLA Modules:
  0.0 90.9 jit_solution(8878363650220780315)
XLA Ops:
  0.7 0.7 add_select_fusion.1
  1.4 0.9 reduce-window.6
  2.3 0.2 slice_reduce_fusion
  2.5 0.1 bitcast_bitcast_fusion
  2.6 2.9 %scatter_custom_fusion = s32[384]{0:T(512)S(1)} fusion(s32[360]{0:T(512)S(1)} %compare_select_fusion.1, s32[360]{0:T(512)S(1)} %get-tuple-element.104, s32[]{:T(128)} %constant.101.clone.1), kind=kCustom, calls=%fused_computation.75 | custom fusion | bytes 1540 | tf_op jit(solution)/shard_map/scatter | solution.py:42
  5.6 0.7 reshape.115
  6.3 6.3 %all-to-all-start = ((s32[4,4,24]{2,1,0:T(4,128)}), s32[4,4,24]{2,1,0:T(4,128)S(1)}, u32[]{:S(2)}, u32[]{:S(2)}) async-start(s32[4,4,24]{2,1,0:T(4,128)} %reshape.115), calls=%async_computation | async-start | bytes 16384 | tf_op jit(solution)/shard_map/all_to_all | solution.py:56
  12.6 3.0 %scatter_custom_fusion.1 = bf16[384,512]{1,0:T(8,128)(2,1)} fusion(s32[360]{0:T(512)S(1)} %compare_select_fusion.1, bf16[360,512]{1,0:T(8,128)(2,1)} %param.5, bf16[]{:T(256)} %constant.100.clone.1), kind=kCustom, calls=%fused_computation.27 | custom fusion | bytes 393728 | tf_op jit(solution)/shard_map/scatter | solution.py:39
  15.6 2.6 %all-to-all-done = s32[4,4,24]{2,1,0:T(4,128)S(1)} async-done(((s32[4,4,24]{2,1,0:T(4,128)}), s32[4,4,24]{2,1,0:T(4,128)S(1)}, u32[]{:S(2)}, u32[]{:S(2)}) %all-to-all-start) | async-done | bytes 1568 | tf_op jit(solution)/shard_map/all_to_all | solution.py:56
  18.2 3.5 %all-to-all-start.2 = ((bf16[4,4,24,512]{3,2,1,0:T(8,128)(2,1)}), bf16[4,4,24,512]{3,2,1,0:T(8,128)(2,1)S(1)}, u32[]{:S(2)}, u32[]{:S(2)}) async-start(bf16[4,4,24,512]{3,2,1,0:T(8,128)(2,1)} %bitcast.5), calls=%async_computation.2 | async-start | bytes 786432 | tf_op jit(solution)/shard_map/all_to_all | solution.py:49
  21.6 0.6 copy.17
  22.2 9.9 %all-to-all-done.2 = bf16[4,4,24,512]{3,2,1,0:T(8,128)(2,1)S(1)} async-done(((bf16[4,4,24,512]{3,2,1,0:T(8,128)(2,1)}), bf16[4,4,24,512]{3,2,1,0:T(8,128)(2,1)S(1)}, u32[]{:S(2)}, u32[]{:S(2)}) %all-to-all-start.2) | async-done | bytes 393248 | tf_op jit(solution)/shard_map/all_to_all | solution.py:49
  32.1 3.2 %all-to-all-start.1 = ((s32[4,4,24]{2,0,1:T(4,128)}), s32[4,4,24]{2,0,1:T(4,128)S(1)}, u32[]{:S(2)}, u32[]{:S(2)}) async-start(s32[4,4,24]{2,0,1:T(4,128)} %copy.17), calls=%async_computation.1 | async-start | bytes 16384 | tf_op jit(solution)/shard_map/all_to_all | solution.py:55
  35.4 0.8 copy.19
  36.2 3.0 %all-to-all-done.1 = s32[4,4,24]{2,0,1:T(4,128)S(1)} async-done(((s32[4,4,24]{2,0,1:T(4,128)}), s32[4,4,24]{2,0,1:T(4,128)S(1)}, u32[]{:S(2)}, u32[]{:S(2)}) %all-to-all-start.1) | async-done | bytes 1568 | tf_op jit(solution)/shard_map/all_to_all | solution.py:55
  39.1 3.5 %all-to-all-start.3 = ((bf16[4,4,24,512]{3,2,0,1:T(8,128)(2,1)}), bf16[4,4,24,512]{3,2,0,1:T(8,128)(2,1)S(1)}, u32[]{:S(2)}, u32[]{:S(2)}) async-start(bf16[4,4,24,512]{3,2,0,1:T(8,128)(2,1)} %copy.19), calls=%async_computation.3 | async-start | bytes 786432 | tf_op jit(solution)/shard_map/all_to_all | solution.py:48
  42.6 0.1 select_n.90
  42.8 7.3 %all-to-all-done.3 = bf16[4,4,24,512]{3,2,0,1:T(8,128)(2,1)S(1)} async-done(((bf16[4,4,24,512]{3,2,0,1:T(8,128)(2,1)}), bf16[4,4,24,512]{3,2,0,1:T(8,128)(2,1)S(1)}, u32[]{:S(2)}, u32[]{:S(2)}) %all-to-all-start.3) | async-done | bytes 393248 | tf_op jit(solution)/shard_map/all_to_all | solution.py:48
  50.1 2.0 %scatter_custom_fusion.2 = bf16[192,512]{1,0:T(8,128)(2,1)S(1)} fusion(s32[384]{0:T(512)S(1)} %fusion.35, bf16[384,512]{1,0:T(8,128)(2,1)S(1)} %bitcast.40, bf16[]{:T(256)} %constant.100.clone.1), kind=kCustom, calls=%fused_computation.29 | custom fusion | bytes 196610 | tf_op jit(solution)/shard_map/scatter | solution.py:67
  52.0 0.1 fusion.15
  52.2 0.1 fusion.16
  52.3 0.1 collective-permute-start
  52.4 8.2 %collective-permute-done = bf16[192,512]{1,0:T(8,128)(2,1)S(1)} collective-permute-done((bf16[192,512]{1,0:T(8,128)(2,1)S(1)}, bf16[192,512]{1,0:T(8,128)(2,1)S(1)}, u32[]{:S(2)}, u32[]{:S(2)}) %collective-permute-start) | collective-permute-done | bytes 196640 | tf_op jit(solution)/shard_map/ppermute | solution.py:74
  60.6 0.0 collective-permute-start.1
  60.6 7.4 %collective-permute-done.1 = bf16[192,512]{1,0:T(8,128)(2,1)S(1)} collective-permute-done((bf16[192,512]{1,0:T(8,128)(2,1)S(1)}, bf16[192,512]{1,0:T(8,128)(2,1)S(1)}, u32[]{:S(2)}, u32[]{:S(2)}) %collective-permute-start.1) | collective-permute-done | bytes 196640 | tf_op jit(solution)/shard_map/ppermute | solution.py:74
  68.0 0.0 collective-permute-start.2
  68.1 7.9 %all_gather.3 = bf16[768,512]{1,0:T(8,128)(2,1)S(1)} all-gather(bf16[192,512]{1,0:T(8,128)(2,1)S(1)} %fusion.16), channel_id=1, replica_groups=mesh['grp'=2,'row'=4,'col'=2,'rep'=2] {'col','rep'}, dimensions={0}, use_global_device_ids=true | all-gather | bytes 983040 | tf_op jit(solution)/shard_map/all_gather | solution.py:70
  76.0 0.0 collective-permute-done.2
  76.0 0.1 constant_dynamic-update-slice_fusion.4
  76.2 0.1 constant_dynamic-update-slice_fusion
  76.3 0.2 constant_dynamic-slice_fusion
  76.5 6.9 %while.12 = (s32[]{:T(128)}, f32[3,256]{1,0:T(4,128)S(1)}, s32[3]{0:T(128)S(1)}, s32[]{:T(128)}, s32[768]{0:T(1024)S(1)}, /*index=5*/bf16[3,256,512]{2,1,0:T(8,1...) while((s32[]{:T(128)}, f32[3,256]{1,0:T(4,128)S(1)}, s32[3]{0:T(128)S(1)}, s32[]{:T(128)}, ...), condition=%wide.region_11.12_spmd, body=%wide.region_7.11_spmd.sunk | while | flops 201916672 | bytes 1595529 | solution.py:101
  76.5 0.7 dynamic_slice.41
  77.9 0.3 fusion.58
  78.2 0.3 fusion.57
  78.5 0.3 fusion.56
  78.8 0.7 dynamic_slice.41
  80.2 0.3 fusion.58
  80.5 0.3 fusion.57
  80.8 0.3 fusion.56
  81.1 0.7 dynamic_slice.41
  82.5 0.3 fusion.58
  82.8 0.3 fusion.57
  83.1 0.3 fusion.56
  83.4 6.8 %pmax.7 = f32[768]{0:T(1024)S(1)} all-reduce(f32[768]{0:T(1024)S(1)} %reshape.119), channel_id=1, replica_groups=mesh['grp'=2,'row'=4,'col'=2,'rep'=2] {'col','rep'}, use_global_device_ids=true, to_apply=%region_12.13 | all-reduce | flops 768 | bytes 6144 | tf_op jit(solution)/shard_map/pmax | solution.py:104
  90.3 0.6 dynamic_slice.20
  (30 shorter events, 0.4 us)
Async XLA Ops:
  6.3 11.9 %all-to-all-start = ((s32[4,4,24]{2,1,0:T(4,128)}), s32[4,4,24]{2,1,0:T(4,128)S(1)}, u32[]{:S(2)}, u32[]{:S(2)}) async-start(s32[4,4,24]{2,1,0:T(4,128)} %reshape.115), calls=%async_computation | async-start | bytes 16384 | tf_op jit(solution)/shard_map/all_to_all | solution.py:56
  18.2 14.0 %all-to-all-start.2 = ((bf16[4,4,24,512]{3,2,1,0:T(8,128)(2,1)}), bf16[4,4,24,512]{3,2,1,0:T(8,128)(2,1)S(1)}, u32[]{:S(2)}, u32[]{:S(2)}) async-start(bf16[4,4,24,512]{3,2,1,0:T(8,128)(2,1)} %bitcast.5), calls=%async_computation.2 | async-start | bytes 786432 | tf_op jit(solution)/shard_map/all_to_all | solution.py:49
  32.1 7.0 %all-to-all-start.1 = ((s32[4,4,24]{2,0,1:T(4,128)}), s32[4,4,24]{2,0,1:T(4,128)S(1)}, u32[]{:S(2)}, u32[]{:S(2)}) async-start(s32[4,4,24]{2,0,1:T(4,128)} %copy.17), calls=%async_computation.1 | async-start | bytes 16384 | tf_op jit(solution)/shard_map/all_to_all | solution.py:55
  39.1 10.9 %all-to-all-start.3 = ((bf16[4,4,24,512]{3,2,0,1:T(8,128)(2,1)}), bf16[4,4,24,512]{3,2,0,1:T(8,128)(2,1)S(1)}, u32[]{:S(2)}, u32[]{:S(2)}) async-start(bf16[4,4,24,512]{3,2,0,1:T(8,128)(2,1)} %copy.19), calls=%async_computation.3 | async-start | bytes 786432 | tf_op jit(solution)/shard_map/all_to_all | solution.py:48
  52.3 8.3 %collective-permute-start = (bf16[192,512]{1,0:T(8,128)(2,1)S(1)}, bf16[192,512]{1,0:T(8,128)(2,1)S(1)}, u32[]{:S(2)}, u32[]{:S(2)}) collective-permute-start(bf16[192,512]{1,0:T(8,128)(2,1)S(1)} %fusion.16), channel_id=1, source_target_pairs={{0,4},{4,8},{8,12},{12,0},{1,5},{5,9},{9,13},{13,1},{2,6},{6,10},{... | collective-permute-start | bytes 589832 | tf_op jit(solution)/shard_map/ppermute | solution.py:74
  60.6 7.5 %collective-permute-start.1 = (bf16[192,512]{1,0:T(8,128)(2,1)S(1)}, bf16[192,512]{1,0:T(8,128)(2,1)S(1)}, u32[]{:S(2)}, u32[]{:S(2)}) collective-permute-start(bf16[192,512]{1,0:T(8,128)(2,1)S(1)} %collective-permute-done), channel_id=1, source_target_pairs={{0,4},{4,8},{8,12},{12,0},{1,5},{5,9},{9,13},{13,1},{2,6},{6,10},{... | collective-permute-start | bytes 589832 | tf_op jit(solution)/shard_map/ppermute | solution.py:74
  68.0 7.9 %collective-permute-start.2 = (bf16[192,512]{1,0:T(8,128)(2,1)S(1)}, bf16[192,512]{1,0:T(8,128)(2,1)S(1)}, u32[]{:S(2)}, u32[]{:S(2)}) collective-permute-start(bf16[192,512]{1,0:T(8,128)(2,1)S(1)} %collective-permute-done.1), channel_id=1, source_target_pairs={{0,4},{4,8},{8,12},{12,0},{1,5},{5,9},{9,13},{13,1},{2,6},{6,10},{... | collective-permute-start | bytes 589832 | tf_op jit(solution)/shard_map/ppermute | solution.py:74
